TPU v7x, 32 devices: a whole 2x2x4 slice. The times are simulated.
32 devices in a mesh: expert: 8 (over z, core), shard: 4 (over y, x).
Axes of the slice: x: 2, y: 2, z: 4, core: 2. Of those that a mesh axis runs over, the one named last changes fastest.
Arguments:
- inputs: float32 [16384, 768], P(('expert', 'shard')), may hold values from -6 to 6
- cotangent: float32 [16384, 768], P(('expert', 'shard')), may hold values from -6 to 6
- norm_one: bfloat16 [768], P('shard'), may hold values from 0.5 to 1.5
- qkv_weight: bfloat16 [768, 2304], P('shard'), may hold values from -0.21875 to 0.21875
- out_weight: bfloat16 [768, 768], P('shard'), may hold values from -3.5 to 3.5
- norm_two: bfloat16 [768], P('shard'), may hold values from 0.5 to 1.5
- shared_gate: bfloat16 [768, 2048], P(None, 'shard'), may hold values from -0.21875 to 0.21875
- shared_up: bfloat16 [768, 2048], P(None, 'shard'), may hold values from -0.21875 to 0.21875
- shared_down: bfloat16 [2048, 768], P('shard'), may hold values from -0.125 to 0.125
- expert_gate: bfloat16 [8, 768, 2048], P('expert'), may hold values from -0.21875 to 0.21875
- expert_up: bfloat16 [8, 768, 2048], P('expert'), may hold values from -0.21875 to 0.21875
- expert_down: bfloat16 [8, 2048, 768], P('expert'), may hold values from -0.125 to 0.125
- gate_weights: float32 [16384, 2], P(('expert', 'shard')), may hold values from 0.25 to 1
- routes: int32 [16384, 2], P(('expert', 'shard')), may hold values from 0 to 7, all different within a row; in each aligned block of 512 rows (0 to 511, 512 to 1023, ...) at most 256 rows name the same one
- prefix: int32 [32], P(('expert', 'shard')), may hold values from 51 to 256
Outputs:
- output: float32 [16384, 768], P(('expert', 'shard'))
- input_grad: float32 [16384, 768], P(('expert', 'shard'))
- norm_one_grad: float32 [768], P('shard')
- qkv_grad: float32 [768, 2304], P('shard')
- out_grad: float32 [768, 768], P('shard')
- norm_two_grad: float32 [768], P('shard')
- shared_gate_grad: float32 [768, 2048], P(None, 'shard')
- shared_up_grad: float32 [768, 2048], P(None, 'shard')
- shared_down_grad: float32 [2048, 768], P('shard')
- expert_gate_grad: float32 [8, 768, 2048], P('expert', None, 'shard')
- expert_up_grad: float32 [8, 768, 2048], P('expert', None, 'shard')
- expert_down_grad: float32 [8, 2048, 768], P('expert', 'shard')
- gate_weights_grad: float32 [16384, 2], P(('expert', 'shard'))
Inputs may be any that keep to these rules, and one draw needn't show every extreme that they name: `routes`: each row names 2 different experts. Among the 512 rows of one device no expert is named more than 256 times, and some device names some expert exactly 256 times. `prefix`: leading tokens of a sequence that all its tokens attend to.
All inputs are finite; a program needn't handle non-finite values.
Results may differ from a plain program's by a relative error of at most 0.02.
Values may be sent and summed in bfloat16 or wider, within the bound.
A program may use at most 256 MiB of HBM per device.

v0:
```python
import jax
import jax.numpy as jnp
from jax import lax
from jax.sharding import PartitionSpec as P

HEADS = 12
HEAD_DIM = 64
TOP = 2
EPS = 1e-06


def rope_tables(length):
    half_dim = HEAD_DIM // 2
    frequency = 10000.0 ** (-jnp.arange(half_dim, dtype=jnp.float32) * 2.0 / HEAD_DIM)
    angles = jnp.arange(length, dtype=jnp.float32)[:, None] * frequency[None, :]
    return (jnp.cos(angles)[:, None, :], jnp.sin(angles)[:, None, :])


def rotate(vectors, cosine_table, sine_table):
    half_dim = vectors.shape[-1] // 2
    first_half = vectors[..., :half_dim]
    second = vectors[..., half_dim:]
    return jnp.concatenate(
        [
            first_half * cosine_table - second * sine_table,
            second * cosine_table + first_half * sine_table,
        ],
        axis=-1,
    )


def gated_unit(pre_gate):
    sigmoid_value = jax.nn.sigmoid(pre_gate)
    activated = pre_gate * sigmoid_value
    derivative = sigmoid_value * (1.0 + pre_gate * (1.0 - sigmoid_value))
    return (activated, derivative)


def norm_back(source, inverse, gain, grad_in):
    scaled = grad_in * gain
    gain_grad = jnp.sum(grad_in * source * inverse, axis=0)
    input_part = inverse * scaled - source * inverse**3 * jnp.mean(
        scaled * source, axis=-1, keepdims=True
    )
    return (gain_grad, input_part)


def matmul(left, right):
    return jnp.dot(left, right, preferred_element_type=jnp.float32)


def on_device(
    inputs,
    cotangent,
    norm_one,
    qkv_weight,
    out_weight,
    norm_two,
    shared_gate,
    shared_up,
    shared_down,
    expert_gate,
    expert_up,
    expert_down,
    gate_weights,
    routes,
    prefix,
):
    length, model_width = inputs.shape
    qkv_full, out_full, gain_one = (
        lax.all_gather(qkv_weight, "shard", axis=0, tiled=True),
        lax.all_gather(out_weight, "shard", axis=0, tiled=True),
        lax.all_gather(norm_one, "shard", axis=0, tiled=True),
    )
    gate_full, up_full, down_full, gain_two = (
        lax.all_gather(shared_gate, "shard", axis=1, tiled=True),
        lax.all_gather(shared_up, "shard", axis=1, tiled=True),
        lax.all_gather(shared_down, "shard", axis=0, tiled=True),
        lax.all_gather(norm_two, "shard", axis=0, tiled=True),
    )
    gain_one = gain_one.astype(jnp.float32)
    gain_two = gain_two.astype(jnp.float32)
    inverse_one = lax.rsqrt(jnp.mean(inputs * inputs, axis=-1, keepdims=True) + EPS)
    normed_one = (inputs * inverse_one * gain_one).astype(jnp.bfloat16)
    projected = matmul(normed_one, qkv_full)
    cosine_table, sine_table = rope_tables(length)
    head_shape = (length, HEADS, HEAD_DIM)
    queries = rotate(
        projected[:, :model_width].reshape(head_shape), cosine_table, sine_table
    ).astype(jnp.bfloat16)
    key_rows = rotate(
        projected[:, model_width : 2 * model_width].reshape(head_shape), cosine_table, sine_table
    ).astype(jnp.bfloat16)
    value_rows = projected[:, 2 * model_width :].reshape(head_shape).astype(jnp.bfloat16)
    score_scale = HEAD_DIM ** (-0.5)
    row_pos = lax.broadcasted_iota(jnp.int32, (length, length), 0)
    col_pos = lax.broadcasted_iota(jnp.int32, (length, length), 1)
    visible = (col_pos < prefix[0]) | (col_pos <= row_pos)

    def masked_scores():
        raw_scores = (
            jnp.einsum("qhd,khd->hqk", queries, key_rows, preferred_element_type=jnp.float32)
            * score_scale
        )
        return jnp.where(visible[None], raw_scores, -1e30)

    scores = masked_scores()
    row_peak = jnp.max(scores, axis=-1, keepdims=True)
    exponent = jnp.exp(scores - row_peak)
    expsum = jnp.sum(exponent, axis=-1, keepdims=True)
    logsum = row_peak + jnp.log(expsum)
    probs_low = (exponent / expsum).astype(jnp.bfloat16)
    attended = (
        jnp.einsum("hqk,khd->qhd", probs_low, value_rows, preferred_element_type=jnp.float32)
        .reshape(length, model_width)
        .astype(jnp.bfloat16)
    )
    resid = inputs + matmul(attended, out_full)
    inverse_two = lax.rsqrt(jnp.mean(resid * resid, axis=-1, keepdims=True) + EPS)
    normed_two = (resid * inverse_two * gain_two).astype(jnp.bfloat16)
    shared_pre = matmul(normed_two, gate_full)
    shared_lift = matmul(normed_two, up_full)
    shared_act, shared_slope = gated_unit(shared_pre)
    shared_hidden = (shared_act * shared_lift).astype(jnp.bfloat16)
    shared_out = matmul(shared_hidden, down_full)
    experts = lax.axis_size("expert") * expert_gate.shape[0]
    capacity = 4 * length // experts
    copies = length * TOP
    flat_route = routes.reshape(copies)
    onehot = (flat_route[:, None] == jnp.arange(experts, dtype=jnp.int32)[None, :]).astype(
        jnp.int32
    )
    slot_index = jnp.sum((jnp.cumsum(onehot, axis=0) - onehot) * onehot, axis=1)
    position = flat_route * capacity + slot_index
    source = (
        jnp.full((experts * capacity,), copies, jnp.int32)
        .at[position]
        .set(jnp.arange(copies, dtype=jnp.int32))
    )
    token_index = jnp.where(source < copies, source // TOP, length)
    copy_index = jnp.where(source < copies, source, copies)

    def place_rows(row_block, index):
        padded = jnp.concatenate([row_block, jnp.zeros((1, model_width), row_block.dtype)], axis=0)
        return padded[index].reshape(experts, capacity, model_width)

    dispatched = place_rows(normed_two, token_index)
    gate_local = expert_gate[0]
    up_local = expert_up[0]
    down_local = expert_down[0]
    received = lax.all_to_all(dispatched, "expert", split_axis=0, concat_axis=0, tiled=True)
    row_count = received.shape[0] * received.shape[1]
    row_block = received.reshape(row_count, model_width)
    pre_gate = matmul(row_block, gate_local)
    pre_up = matmul(row_block, up_local)
    activated, unused_slope = gated_unit(pre_gate)
    hidden = (activated * pre_up).astype(jnp.bfloat16)
    result = matmul(hidden, down_local).astype(jnp.bfloat16).reshape(received.shape)
    returned = lax.all_to_all(result, "expert", split_axis=0, concat_axis=0, tiled=True)
    hidden_shape = (received.shape[0], received.shape[1], pre_gate.shape[1])
    outcome = (returned, received, pre_gate.reshape(hidden_shape), pre_up.reshape(hidden_shape))
    returned, kept_rows, kept_gate, kept_up = outcome
    picked = (
        returned.reshape(experts * capacity, model_width)[position]
        .astype(jnp.float32)
        .reshape(length, TOP, model_width)
    )
    mixture = jnp.sum(gate_weights[:, :, None] * picked, axis=1)
    output = resid + mixture + shared_out
    gate_weights_grad = jnp.sum(cotangent[:, None, :] * picked, axis=2)
    copy_grad = (
        (gate_weights[:, :, None] * cotangent[:, None, :])
        .astype(jnp.bfloat16)
        .reshape(copies, model_width)
    )
    grad_send = place_rows(copy_grad, copy_index)
    grad_recv = lax.all_to_all(grad_send, "expert", split_axis=0, concat_axis=0, tiled=True)
    row_count = kept_rows.shape[0] * kept_rows.shape[1]
    rows_flat = kept_rows.reshape(row_count, model_width)
    pre_gate = kept_gate.reshape(row_count, -1)
    pre_up = kept_up.reshape(row_count, -1)
    grad_flat = grad_recv.reshape(row_count, model_width)
    activated, derivative = gated_unit(pre_gate)
    hidden_grad = matmul(grad_flat, down_local.T)
    gate_pre_grad = (hidden_grad * pre_up * derivative).astype(jnp.bfloat16)
    up_pre_grad = (hidden_grad * activated).astype(jnp.bfloat16)
    row_grad = (
        (matmul(gate_pre_grad, gate_local.T) + matmul(up_pre_grad, up_local.T))
        .astype(jnp.bfloat16)
        .reshape(kept_rows.shape)
    )
    row_returned = lax.all_to_all(row_grad, "expert", split_axis=0, concat_axis=0, tiled=True)
    hidden = (activated * pre_up).astype(jnp.bfloat16)
    gate_term = matmul(rows_flat.T, gate_pre_grad)
    up_term = matmul(rows_flat.T, up_pre_grad)
    down_term = matmul(hidden.T, grad_flat)
    expert_gate_grad, expert_up_grad, expert_down_grad = (
        lax.psum_scatter(
            gate_term[None].astype(jnp.bfloat16), "shard", scatter_dimension=2, tiled=True
        ).astype(jnp.float32),
        lax.psum_scatter(
            up_term[None].astype(jnp.bfloat16), "shard", scatter_dimension=2, tiled=True
        ).astype(jnp.float32),
        lax.psum_scatter(
            down_term[None].astype(jnp.bfloat16), "shard", scatter_dimension=1, tiled=True
        ).astype(jnp.float32),
    )
    copy_back = (
        row_returned.reshape(experts * capacity, model_width)[position]
        .astype(jnp.float32)
        .reshape(length, TOP, model_width)
    )
    out_low = cotangent.astype(jnp.bfloat16)
    shared_down_grad = matmul(shared_hidden.T, out_low)
    shared_hgrad = matmul(out_low, down_full.T)
    shared_pre_grad = (shared_hgrad * shared_lift * shared_slope).astype(jnp.bfloat16)
    shared_lift_grad = (shared_hgrad * shared_act).astype(jnp.bfloat16)
    shared_gate_grad = matmul(normed_two.T, shared_pre_grad)
    shared_up_grad = matmul(normed_two.T, shared_lift_grad)
    normed_two_grad = (
        matmul(shared_pre_grad, gate_full.T)
        + matmul(shared_lift_grad, up_full.T)
        + jnp.sum(copy_back, axis=1)
    )
    gain_two_grad, resid_extra = norm_back(resid, inverse_two, gain_two, normed_two_grad)
    resid_grad = cotangent + resid_extra
    ffn_pieces = (
        lax.psum_scatter(
            shared_gate_grad.astype(jnp.bfloat16), "shard", scatter_dimension=1, tiled=True
        ).astype(jnp.float32),
        lax.psum_scatter(
            shared_up_grad.astype(jnp.bfloat16), "shard", scatter_dimension=1, tiled=True
        ).astype(jnp.float32),
        lax.psum_scatter(
            shared_down_grad.astype(jnp.bfloat16), "shard", scatter_dimension=0, tiled=True
        ).astype(jnp.float32),
        lax.psum_scatter(
            gain_two_grad.astype(jnp.bfloat16), "shard", scatter_dimension=0, tiled=True
        ).astype(jnp.float32),
    )
    attn_low = resid_grad.astype(jnp.bfloat16)
    out_weight_grad = matmul(attended.T, attn_low)
    attended_grad = matmul(attn_low, out_full.T).astype(jnp.bfloat16).reshape(head_shape)
    scores = masked_scores()
    probs_full = jnp.exp(scores - logsum)
    value_grad = jnp.einsum(
        "hqk,qhd->khd",
        probs_full.astype(jnp.bfloat16),
        attended_grad,
        preferred_element_type=jnp.float32,
    )
    probs_grad = jnp.einsum(
        "qhd,khd->hqk", attended_grad, value_rows, preferred_element_type=jnp.float32
    )
    score_grad = (
        probs_full * (probs_grad - jnp.sum(probs_full * probs_grad, axis=-1, keepdims=True))
    ).astype(jnp.bfloat16)
    query_grad = (
        jnp.einsum("hqk,khd->qhd", score_grad, key_rows, preferred_element_type=jnp.float32)
        * score_scale
    )
    key_grad = (
        jnp.einsum("hqk,qhd->khd", score_grad, queries, preferred_element_type=jnp.float32)
        * score_scale
    )
    projected_grad = jnp.concatenate(
        [
            rotate(query_grad, cosine_table, -sine_table).reshape(length, model_width),
            rotate(key_grad, cosine_table, -sine_table).reshape(length, model_width),
            value_grad.reshape(length, model_width),
        ],
        axis=1,
    ).astype(jnp.bfloat16)
    qkv_weight_grad = matmul(normed_one.T, projected_grad)
    normed_one_grad = matmul(projected_grad, qkv_full.T)
    gain_one_grad, input_extra = norm_back(inputs, inverse_one, gain_one, normed_one_grad)
    input_grad = resid_grad + input_extra
    attn_pieces = (
        lax.psum_scatter(
            qkv_weight_grad.astype(jnp.bfloat16), "shard", scatter_dimension=0, tiled=True
        ).astype(jnp.float32),
        lax.psum_scatter(
            out_weight_grad.astype(jnp.bfloat16), "shard", scatter_dimension=0, tiled=True
        ).astype(jnp.float32),
        lax.psum_scatter(
            gain_one_grad.astype(jnp.bfloat16), "shard", scatter_dimension=0, tiled=True
        ).astype(jnp.float32),
    )
    summed = (
        lax.psum(attn_pieces[0].astype(jnp.bfloat16), "expert").astype(jnp.float32),
        lax.psum(attn_pieces[1].astype(jnp.bfloat16), "expert").astype(jnp.float32),
        lax.psum(attn_pieces[2].astype(jnp.bfloat16), "expert").astype(jnp.float32),
        lax.psum(ffn_pieces[0].astype(jnp.bfloat16), "expert").astype(jnp.float32),
        lax.psum(ffn_pieces[1].astype(jnp.bfloat16), "expert").astype(jnp.float32),
        lax.psum(ffn_pieces[2].astype(jnp.bfloat16), "expert").astype(jnp.float32),
        lax.psum(ffn_pieces[3].astype(jnp.bfloat16), "expert").astype(jnp.float32),
    )
    return (
        output,
        input_grad,
        summed[2],
        summed[0],
        summed[1],
        summed[6],
        summed[3],
        summed[4],
        summed[5],
        expert_gate_grad,
        expert_up_grad,
        expert_down_grad,
        gate_weights_grad,
    )


def solution(mesh):
    in_specs = (
        P(("expert", "shard"), None),
        P(("expert", "shard"), None),
        P("shard"),
        P("shard", None),
        P("shard", None),
        P("shard"),
        P(None, "shard"),
        P(None, "shard"),
        P("shard", None),
        P("expert", None, None),
        P("expert", None, None),
        P("expert", None, None),
        P(("expert", "shard"), None),
        P(("expert", "shard"), None),
        P(("expert", "shard")),
    )
    out_specs = (
        P(("expert", "shard"), None),
        P(("expert", "shard"), None),
        P("shard"),
        P("shard", None),
        P("shard", None),
        P("shard"),
        P(None, "shard"),
        P(None, "shard"),
        P("shard", None),
        P("expert", None, "shard"),
        P("expert", None, "shard"),
        P("expert", "shard", None),
        P(("expert", "shard"), None),
    )
    return jax.shard_map(
        on_device, mesh=mesh, in_specs=in_specs, out_specs=out_specs, check_vma=False
    )
```

profile of v0, /device:TPU:0, one launch (start us, length us, event | category | flops | bytes accessed | tf_op | source)
XLA Modules:
  0.0 837.4 jit_solution(5135879969428653697)
XLA Ops:
  34.1 11.7 %gather_fusion.2 = bf16[2048,768]{1,0:T(8,128)(2,1)} fusion(bf16[1025,768]{1,0:T(8,128)(2,1)} %concatenate.29, s32[2048]{0:T(1024)S(1)} %get-tuple-element.63), kind=kCustom, calls=%fused_computation.2 | custom fusion | bytes 6299648 | tf_op jit(solution)/shard_map/gather | solution.py:145
  54.9 10.7 %all-reduce.9 = (bf16[768]{0:T(1024)(128)(2,1)S(1)}, bf16[768]{0:T(1024)(128)(2,1)}) all-reduce(bf16[768]{0:T(1024)(128)(2,1)S(1)} %dynamic-update-slice, bf16[768]{0:T(1024)(128)(2,1)S(1)} %dynamic-update-slice.1), channel_id=1, replica_groups=mesh['expert'=8,'shard'=4] {'shard'}, use_global_device_ids=true, to_apply=%add.2 | all-reduce | flops 1536 | bytes 6144
  116.9 18.3 %all-gather.10.cloned.1.call-done = bf16[768,2048]{1,0:T(8,128)(2,1)} async-done(((bf16[768,512]{1,0:T(8,128)(2,1)}), bf16[768,2048]{1,0:T(8,128)(2,1)}) %all-gather.10.cloned.1.call-update) | async-done | bytes 3145744 | tf_op jit(solution)/shard_map/all_gather | solution.py:76
  141.1 39.6 %all-gather.12.cloned.1.call-done = bf16[768,2048]{1,0:T(8,128)(2,1)} async-done(((bf16[768,512]{1,0:T(8,128)(2,1)}), bf16[768,2048]{1,0:T(8,128)(2,1)}) %all-gather.12.cloned.1.call-update) | async-done | bytes 3145744 | tf_op jit(solution)/shard_map/all_gather | solution.py:77
  186.7 39.8 %all-gather.14.cloned.1.call-done = bf16[2048,768]{1,0:T(8,128)(2,1)} async-done(((bf16[512,768]{1,0:T(8,128)(2,1)}), bf16[2048,768]{1,0:T(8,128)(2,1)}) %all-gather.14.cloned.1.call-update) | async-done | bytes 3145744 | tf_op jit(solution)/shard_map/all_gather | solution.py:78
  226.4 10.0 %multiply_convert_fusion.4 = (bf16[512,2048]{1,0:T(8,128)(2,1)}, bf16[512,2048]{1,0:T(8,128)(2,1)S(1)}, bf16[512,2048]{1,0:T(8,128)(2,1)}) fusion(f32[512,2048]{1,0:T(8,128)} %fusion.62, f32[512,2048]{1,0:T(8,128)} %fusion.63, bf16[2048,768]{1,0:T(8,128)(2,1)} %all-gather.14.cloned.1.call-done, f32[512,768]{1,0:T(8,128)} %param.16), kind=kOutput, calls=%fused_computation.24 | convolution fusion | flops 1626734592 | bytes 19398656 | tf_op jit(solution)/shard_map/dot_general | solution.py:49
  243.3 11.4 %gather_fusion = bf16[2048,768]{1,0:T(8,128)(2,1)} fusion(bf16[513,768]{1,0:T(8,128)(2,1)} %concatenate.28, s32[2048]{0:T(1024)S(1)} %get-tuple-element.64), kind=kCustom, calls=%fused_computation | custom fusion | bytes 6299648 | tf_op jit(solution)/shard_map/gather | solution.py:145
  264.8 12.8 %fusion.9 = f32[2048,2048]{1,0:T(8,128)} fusion(bf16[2048,768]{1,0:T(8,128)(2,1)} %bitcast.18, bf16[1,2048,768]{2,1,0:T(8,128)(2,1)} %param.26), kind=kOutput, calls=%fused_computation.36 | convolution fusion | flops 6442450944 | bytes 23068672 | tf_op jit(solution)/shard_map/dot_general | solution.py:49
  277.6 53.3 %all-to-all-done = bf16[8,256,768]{2,1,0:T(8,128)(2,1)} async-done(((bf16[8,256,768]{2,1,0:T(8,128)(2,1)}), bf16[8,256,768]{2,1,0:T(8,128)(2,1)}, u32[]{:S(2)}, u32[]{:S(2)}) %all-to-all-start) | async-done | bytes 3145760 | tf_op jit(solution)/shard_map/all_to_all | solution.py:151
  330.9 12.6 %fusion.14 = f32[2048,2048]{1,0:T(8,128)} fusion(bf16[2048,768]{1,0:T(8,128)(2,1)} %bitcast.11, bf16[1,768,2048]{2,1,0:T(8,128)(2,1)} %param.25), kind=kOutput, calls=%fused_computation.41 | convolution fusion | flops 6442450944 | bytes 23068672 | tf_op jit(solution)/shard_map/dot_general | solution.py:49
  343.5 26.2 %multiply_convert_fusion.1 = (bf16[2048,2048]{1,0:T(8,128)(2,1)}, bf16[2048,2048]{1,0:T(8,128)(2,1)}, bf16[2048,2048]{1,0:T(8,128)(2,1)}) fusion(f32[2048,2048]{1,0:T(8,128)} %fusion.9, f32[2048,2048]{1,0:T(8,128)} %fusion.14, bf16[2048,768]{1,0:T(8,128)(2,1)} %bitcast.11, bf16[1,768,2048]{2,1,0:T(8,128)(2,1)S(1)} %copy-done), kind=kOutput, calls=%fused_computation.6 | convolution fusion | flops 6505365504 | bytes 65011712 | tf_op jit(solution)/shard_map/dot_general | solution.py:49
  369.7 10.4 %fusion.12 = f32[2048,768]{1,0:T(8,128)S(1)} fusion(bf16[2048,2048]{1,0:T(8,128)(2,1)} %get-tuple-element.44, bf16[1,768,2048]{2,1,0:T(8,128)(2,1)} %param.25), kind=kOutput, calls=%fused_computation.39 | convolution fusion | flops 6442450944 | bytes 17825792 | tf_op jit(solution)/shard_map/dot_general | solution.py:49
  403.9 59.5 %all-to-all-done.3 = bf16[8,256,768]{2,1,0:T(8,128)(2,1)S(1)} async-done(((bf16[8,256,768]{2,1,0:T(8,128)(2,1)}), bf16[8,256,768]{2,1,0:T(8,128)(2,1)S(1)}, u32[]{:S(2)}, u32[]{:S(2)}) %all-to-all-start.3) | async-done | bytes 3145760 | tf_op jit(solution)/shard_map/all_to_all | solution.py:192
  493.2 11.4 %multiply_reduce_fusion = (f32[12,512]{1,0:T(8,128)S(1)}, f32[12,512,512]{1,2,0:T(8,128)}) fusion(f32[12,512]{1,0:T(8,128)S(1)} %log_add_fusion, f32[12,512,512]{1,2,0:T(8,128)} %get-tuple-element.75, pred[512,512]{0,1:T(8,128)(4,1)S(1)} %copy-done.13, bf16[512,12,64]{0,2,1:T(8,128)(2,1)} %bitcast.126, bf16[512,12,64]{0,2,1:T(8,128)(2,1)S(1)} %bitcast.125), kind=kOutput, calls=%fused_computation.11 | convolution fusion | flops 418375680 | bytes 27049984 | tf_op jit(solution)/shard_map/qhd,khd->hqk/dot_general | solution.py:252
  506.0 10.1 %multiply_convert_fusion.3 = bf16[12,512,512]{1,2,0:T(8,128)(2,1)} fusion(f32[12,512,512]{1,2,0:T(8,128)} %get-tuple-element.80, f32[12,512]{1,0:T(8,128)S(1)} %get-tuple-element.79, f32[12,512]{1,0:T(8,128)S(1)} %log_add_fusion, f32[12,512,512]{1,2,0:T(8,128)S(1)} %bitcast.115, pred[512,512]{0,1:T(8,128)(4,1)S(1)} %copy-done.13), kind=kLoop, calls=%fused_computation.10 | loop fusion | flops 18874368 | bytes 31768576 | tf_op jit(solution)/shard_map/convert_element_type | solution.py:257
  533.1 12.2 %fusion.21 = bf16[1,768,2048]{2,1,0:T(8,128)(2,1)} fusion(bf16[2048,768]{1,0:T(8,128)(2,1)} %bitcast.11, bf16[2048,2048]{1,0:T(8,128)(2,1)} %get-tuple-element.43), kind=kOutput, calls=%fused_computation.51 | convolution fusion | flops 6444023808 | bytes 14680064 | tf_op jit(solution)/shard_map/dot_general | solution.py:49
  545.4 12.2 %fusion.22 = bf16[1,768,2048]{2,1,0:T(8,128)(2,1)} fusion(bf16[2048,768]{1,0:T(8,128)(2,1)} %bitcast.11, bf16[2048,2048]{1,0:T(8,128)(2,1)} %get-tuple-element.44), kind=kOutput, calls=%fused_computation.52 | convolution fusion | flops 6444023808 | bytes 14680064 | tf_op jit(solution)/shard_map/dot_general | solution.py:49
  557.7 11.6 %fusion.20 = bf16[1,2048,768]{2,1,0:T(8,128)(2,1)} fusion(bf16[2048,2048]{1,0:T(8,128)(2,1)} %get-tuple-element.45, bf16[2048,768]{1,0:T(8,128)(2,1)} %bitcast.18), kind=kOutput, calls=%fused_computation.50 | convolution fusion | flops 6444023808 | bytes 14680064 | tf_op jit(solution)/shard_map/dot_general | solution.py:49
  571.2 10.2 %convolution_convert_fusion.3 = bf16[2048,768]{1,0:T(8,128)(2,1)} fusion(bf16[2048,2048]{1,0:T(8,128)(2,1)} %get-tuple-element.45, bf16[1,2048,768]{2,1,0:T(8,128)(2,1)S(1)} %copy-done.58), kind=kOutput, calls=%fused_computation.31 | convolution fusion | flops 6444023808 | bytes 14680064 | tf_op jit(solution)/shard_map/dot_general | solution.py:49
  585.8 70.8 %all-to-all-done.1 = bf16[8,256,768]{2,1,0:T(8,128)(2,1)S(1)} async-done(((bf16[8,256,768]{2,1,0:T(8,128)(2,1)}), bf16[8,256,768]{2,1,0:T(8,128)(2,1)S(1)}, u32[]{:S(2)}, u32[]{:S(2)}) %all-to-all-start.1) | async-done | bytes 3145760 | tf_op jit(solution)/shard_map/all_to_all | solution.py:159
  682.0 13.6 %all-reduce.6 = (bf16[192]{0:T(256)(128)(2,1)S(1)}, bf16[192]{0:T(256)(128)(2,1)S(1)}) all-reduce(bf16[192]{0:T(256)(128)(2,1)S(1)} %dynamic-slice.3, bf16[192]{0:T(256)(128)(2,1)S(1)} %dynamic-slice.5), channel_id=1, replica_groups=mesh['expert'=8,'shard'=4] {'expert'}, use_global_device_ids=true, to_apply=%region_15.16 | all-reduce | flops 384 | bytes 1536 | tf_op jit(solution)/shard_map/psum | solution.py:292
  696.8 9.7 %multiply_reduce_fusion.1 = (f32[512,2]{1,0:T(8,128)}, f32[512,768]{1,0:T(8,128)}) fusion(f32[512,2,768]{2,1,0:T(2,128)} %reshape.293, f32[512,768]{1,0:T(8,128)} %param.16, f32[512,2]{1,0:T(8,128)S(1)} %copy-done.19), kind=kLoop, calls=%fused_computation.47 | loop fusion | flops 2751488 | bytes 6299648 | tf_op jit(solution)/shard_map/reduce_sum | solution.py:170
  721.8 11.9 %reduce-scatter.23.cloned.1.call-done = bf16[1,512,768]{2,1,0:T(8,128)(2,1)} async-done(((bf16[1,2048,768]{2,1,0:T(8,128)(2,1)}), bf16[1,512,768]{2,1,0:T(8,128)(2,1)}) %reduce-scatter.23.cloned.1.call-update) | async-done | bytes 786448 | tf_op jit(solution)/shard_map/reduce_scatter | solution.py:204
  736.1 85.9 %all-reduce.12.cloned.1.call-done = (bf16[192,2304]{1,0:T(8,128)(2,1)}, bf16[192,768]{1,0:T(8,128)(2,1)}, bf16[768,512]{1,0:T(8,128)(2,1)}, bf16[768,512]{1,0:T(8,128)(2,1)}, bf16[512,768]{1,0:T(8,128)(2,1)}) async-done(((bf16[192,2304]{1,0:T(8,128)(2,1)}, bf16[192,768]{1,0:T(8,128)(2,1)}, bf16[768,512]{1,0:T(8,128)(2,1)}, bf16[768,512]{1,0:T(8,128)(2,1)}, bf16[512,768]{1,0:T(8,128)(2,1)}), ...) | async-done | bytes 3538960 | tf_op jit(solution)/shard_map/psum | solution.py:290
  (279 shorter events, 244.5 us)
Async XLA Ops:
  7.2 336.3 %copy-start = (bf16[1,768,2048]{2,1,0:T(8,128)(2,1)S(1)}, bf16[1,768,2048]{2,1,0:T(8,128)(2,1)}, u32[]{:S(2)}) copy-start(bf16[1,768,2048]{2,1,0:T(8,128)(2,1)} %param.24) | copy-start | bytes 9437188
  7.2 63.0 %all-gather.6.cloned.1.call-start = ((), (), s32[]{:S(2)}) async-start(), calls=%async_computation.12 | async-start | bytes 4423680 | tf_op jit(solution)/shard_map/all_gather | solution.py:71
  7.9 103.7 %all-gather.8.cloned.1.call-start = ((), (), s32[]{:S(2)}) async-start(), calls=%async_computation.13 | async-start | bytes 1474560 | tf_op jit(solution)/shard_map/all_gather | solution.py:72
  8.7 126.5 %all-gather.10.cloned.1.call-start = ((), (), s32[]{:S(2)}) async-start(), calls=%async_computation.14 | async-start | bytes 3932160 | tf_op jit(solution)/shard_map/all_gather | solution.py:76
  9.4 171.3 %all-gather.12.cloned.1.call-start = ((), (), s32[]{:S(2)}) async-start(), calls=%async_computation.15 | async-start | bytes 3932160 | tf_op jit(solution)/shard_map/all_gather | solution.py:77
  45.8 208.9 %all-to-all-start.2 = ((bf16[8,256,768]{2,1,0:T(8,128)(2,1)}), bf16[8,256,768]{2,1,0:T(8,128)(2,1)}, u32[]{:S(2)}, u32[]{:S(2)}) async-start(bf16[8,256,768]{2,1,0:T(8,128)(2,1)} %bitcast.120), calls=%async_computation.2 | async-start | bytes 6291456 | tf_op jit(solution)/shard_map/all_to_all | solution.py:177
  52.4 174.0 %all-gather.14.cloned.1.call-start = ((), (), s32[]{:S(2)}) async-start(), calls=%async_computation.16 | async-start | bytes 3932160 | tf_op jit(solution)/shard_map/all_gather | solution.py:78
  53.0 643.7 %reduce-scatter.13.cloned.1.call-start = ((), (), s32[]{:S(2)}) async-start(), calls=%async_computation.19 | async-start | bytes 3932160 | tf_op jit(solution)/shard_map/reduce_scatter | solution.py:228
  68.6 36.3 %copy-start.12 = (pred[512,512]{0,1:T(8,128)(4,1)}, pred[512,512]{0,1:T(8,128)(4,1)S(1)}, u32[]{:S(2)}) copy-start(pred[512,512]{0,1:T(8,128)(4,1)S(1)} %fusion.29) | copy-start | bytes 786436
  69.5 14.5 %copy-start.37 = (f32[512,32]{0,1:T(8,128)}, f32[512,32]{0,1:T(8,128)S(1)}, u32[]{:S(2)}) copy-start(f32[512,32]{0,1:T(8,128)S(1)} %get-tuple-element.73) | copy-start | bytes 196612
  70.2 45.1 %copy-start.44 = (f32[768]{0:T(1024)}, f32[768]{0:T(1024)S(1)}, u32[]{:S(2)}) copy-start(f32[768]{0:T(1024)S(1)} %convert_element_type.190) | copy-start | bytes 9220
  254.7 76.2 %all-to-all-start = ((bf16[8,256,768]{2,1,0:T(8,128)(2,1)}), bf16[8,256,768]{2,1,0:T(8,128)(2,1)}, u32[]{:S(2)}, u32[]{:S(2)}) async-start(bf16[8,256,768]{2,1,0:T(8,128)(2,1)} %bitcast.121), calls=%async_computation | async-start | bytes 6291456 | tf_op jit(solution)/shard_map/all_to_all | solution.py:151
  259.3 437.4 %reduce-scatter.15.cloned.1.call-start = ((), (), s32[]{:S(2)}) async-start(), calls=%async_computation.20 | async-start | bytes 3932160 | tf_op jit(solution)/shard_map/reduce_scatter | solution.py:231
  388.3 75.1 %all-to-all-start.3 = ((bf16[8,256,768]{2,1,0:T(8,128)(2,1)}), bf16[8,256,768]{2,1,0:T(8,128)(2,1)S(1)}, u32[]{:S(2)}, u32[]{:S(2)}) async-start(bf16[8,256,768]{2,1,0:T(8,128)(2,1)} %bitcast.130), calls=%async_computation.3 | async-start | bytes 6291456 | tf_op jit(solution)/shard_map/all_to_all | solution.py:192
  392.0 304.7 %reduce-scatter.17.cloned.1.call-start = ((), (), s32[]{:S(2)}) async-start(), calls=%async_computation.21 | async-start | bytes 3932160 | tf_op jit(solution)/shard_map/reduce_scatter | solution.py:234
  397.6 299.1 %reduce-scatter.11.cloned.1.call-start = ((), (), s32[]{:S(2)}) async-start(), calls=%async_computation.18 | async-start | bytes 1474560 | tf_op jit(solution)/shard_map/reduce_scatter | solution.py:282
  493.2 12.8 %slice-start.2 = ((s8[12582912]{0:T(1024)(128)(4,1)}), s8[4194304]{0:T(1024)(128)(4,1)S(1)}, s32[]{:S(2)}) async-start(s8[12582912]{0:T(1024)(128)(4,1)} %bitcast.114), calls=%async_computation.28 | async-start | bytes 8388608
  516.1 180.6 %reduce-scatter.9.cloned.1.call-start = ((), (), s32[]{:S(2)}) async-start(), calls=%async_computation.17 | async-start | bytes 4423680 | tf_op jit(solution)/shard_map/reduce_scatter | solution.py:279
  533.1 183.7 %reduce-scatter.19.cloned.1.call-start = ((), (), s32[]{:S(2)}) async-start(), calls=%async_computation.22 | async-start | bytes 3932160 | tf_op jit(solution)/shard_map/reduce_scatter | solution.py:198
  545.3 174.0 %reduce-scatter.21.cloned.1.call-start = ((), (), s32[]{:S(2)}) async-start(), calls=%async_computation.23 | async-start | bytes 3932160 | tf_op jit(solution)/shard_map/reduce_scatter | solution.py:201
  557.6 176.1 %reduce-scatter.23.cloned.1.call-start = ((), (), s32[]{:S(2)}) async-start(), calls=%async_computation.24 | async-start | bytes 3932160 | tf_op jit(solution)/shard_map/reduce_scatter | solution.py:204
  581.5 75.1 %all-to-all-start.1 = ((bf16[8,256,768]{2,1,0:T(8,128)(2,1)}), bf16[8,256,768]{2,1,0:T(8,128)(2,1)S(1)}, u32[]{:S(2)}, u32[]{:S(2)}) async-start(bf16[8,256,768]{2,1,0:T(8,128)(2,1)} %bitcast.131), calls=%async_computation.1 | async-start | bytes 6291456 | tf_op jit(solution)/shard_map/all_to_all | solution.py:159
  585.1 236.8 %all-reduce.12.cloned.1.call-start = ((), (), s32[]{:S(2)}) async-start(), calls=%async_computation.25 | async-start | bytes 7077888 | tf_op jit(solution)/shard_map/psum | solution.py:290
  672.7 24.1 %copy-start.19 = (f32[512,2]{1,0:T(8,128)S(1)}, f32[512,2]{1,0:T(8,128)}, u32[]{:S(2)}) copy-start(f32[512,2]{1,0:T(8,128)} %copy-done.18) | copy-start | bytes 12292
  (65 other events, 345.6 us)
Sparse Core Ops, SparseCore 0:
  9.9 49.9 all-gather.5
  61.7 27.7 all-gather.7
  91.3 43.8 all-gather.9
  136.8 43.8 all-gather.11
  182.4 43.9 all-gather.13
  241.4 43.9 reduce-scatter.12
  288.3 43.9 reduce-scatter.14
  397.7 44.3 reduce-scatter.16
  516.3 26.4 reduce-scatter.10
  545.7 47.2 reduce-scatter.8
  595.9 43.9 reduce-scatter.18
  642.7 44.1 reduce-scatter.20
  689.9 43.7 reduce-scatter.22
  736.3 85.5 all-reduce.11
where the time goes:
time: 845 us; the launch traced here: 837 us
  waiting for transfers between devices  382 us (45%)
  matrix products  222 us (26%)
  local copies, waits for them, and re-layouts  96.1 us (11%)
  other arithmetic  67.4 us (8%)
  blocking collectives  33.4 us (4%)
  starting transfers between devices  19.1 us (2%)
  between operations  17.1 us (2%)
    dot_general x24, matrix products, matmul(): return jnp.dot(left, right, preferred_element_type=jnp.float32)  190 us
    psum x1, waiting for transfers between devices, on_device(): lax.psum(attn_pieces[0].astype(jnp.bfloat16), 'expert').astype(jnp.float32)  85.9 us
    all_to_all x1, waiting for transfers between devices, on_device(): lax.all_to_all(result, 'expert', split_axis=0, concat_axis=0, tiled=True)  70.8 us
    all_to_all x1, waiting for transfers between devices, on_device(): lax.all_to_all(row_grad, 'expert', split_axis=0, concat_axis=0, tiled=True)  59.5 us
    all_to_all x1, waiting for transfers between devices, on_device(): lax.all_to_all(dispatched, 'expert', split_axis=0, concat_axis=0, tiled=T...  53.3 us
    all_gather x1, waiting for transfers between devices, on_device(): lax.all_gather(shared_down, 'shard', axis=0, tiled=True)  39.8 us
    all_gather x1, waiting for transfers between devices, on_device(): lax.all_gather(shared_up, 'shard', axis=1, tiled=True)  39.6 us
    gather x2, local copies, waits for them, and re-layouts, place_rows(): return padded[index].reshape(experts, capacity, model_width)  23 us
  transfers between devices with their start and end apart: 18, of which 8 were waited for; matrix products, arithmetic and copies ran while one was open for 43% of the time, Pallas kernels for 0%

commit v1 on v0

--- a/solution.py
+++ b/solution.py
@@ -287,7 +287,9 @@
         ).astype(jnp.float32),
     )
     summed = (
-        lax.psum(attn_pieces[0].astype(jnp.bfloat16), "expert").astype(jnp.float32),
+        jnp.sum(lax.all_gather(attn_pieces[0].astype(jnp.bfloat16), "expert"), axis=0).astype(
+            jnp.float32
+        ),
         lax.psum(attn_pieces[1].astype(jnp.bfloat16), "expert").astype(jnp.float32),
         lax.psum(attn_pieces[2].astype(jnp.bfloat16), "expert").astype(jnp.float32),
         lax.psum(ffn_pieces[0].astype(jnp.bfloat16), "expert").astype(jnp.float32),

time: 845 us -> 901 us (1.066)
  waiting for transfers between devices: 382 us -> 433 us
    all_gather x0 -> x1, waiting for transfers between devices: none -> 65.3 us  [on_device(): lax.all_gather(attn_pieces[0].astype(jnp.bfloat16), 'expert')]
    psum x1, waiting for transfers between devices: 85.9 us -> 59.7 us  [on_device(): lax.psum(attn_pieces[1].astype(jnp.bfloat16), 'expert').astype(jnp.float32)]
    reduce_scatter x1, waiting for transfers between devices: 0.02 us -> 23.1 us  [on_device(): lax.psum_scatter(qkv_weight_grad.astype(jnp.bfloat16), 'shard', scatter_d...]
    reduce_scatter x1, waiting for transfers between devices: 11.9 us -> 0.01 us  [on_device(): lax.psum_scatter(down_term[None].astype(jnp.bfloat16), 'shard', scatter_d...]
  transfers between devices with their start and end apart: 18 -> 19, of which waited for: 8 -> 9; matrix products, arithmetic and copies ran while one was open for 43% -> 41% of each run, Pallas kernels for 0% -> 0%
where the time goes in v1:
time: 901 us; the launch traced here: 894 us
  waiting for transfers between devices  433 us (48%)
  matrix products  222 us (25%)
  local copies, waits for them, and re-layouts  94 us (10%)
  other arithmetic  73.9 us (8%)
  blocking collectives  33.4 us (4%)
  starting transfers between devices  20.4 us (2%)
  between operations  17.1 us (2%)
    dot_general x24, matrix products, matmul(): return jnp.dot(left, right, preferred_element_type=jnp.float32)  190 us
    all_to_all x1, waiting for transfers between devices, on_device(): lax.all_to_all(result, 'expert', split_axis=0, concat_axis=0, tiled=True)  70.8 us
    all_gather x1, waiting for transfers between devices, on_device(): lax.all_gather(attn_pieces[0].astype(jnp.bfloat16), 'expert')  65.3 us
    psum x1, waiting for transfers between devices, on_device(): lax.psum(attn_pieces[1].astype(jnp.bfloat16), 'expert').astype(jnp.float32)  59.7 us
    all_to_all x1, waiting for transfers between devices, on_device(): lax.all_to_all(row_grad, 'expert', split_axis=0, concat_axis=0, tiled=True)  59.5 us
    all_to_all x1, waiting for transfers between devices, on_device(): lax.all_to_all(dispatched, 'expert', split_axis=0, concat_axis=0, tiled=T...  53.1 us
    all_gather x1, waiting for transfers between devices, on_device(): lax.all_gather(shared_down, 'shard', axis=0, tiled=True)  39.8 us
    all_gather x1, waiting for transfers between devices, on_device(): lax.all_gather(shared_up, 'shard', axis=1, tiled=True)  39.6 us
  transfers between devices with their start and end apart: 19, of which 9 were waited for; matrix products, arithmetic and copies ran while one was open for 41% of the time, Pallas kernels for 0%

profile of v1, /device:TPU:0, one launch (start us, length us, event | category | flops | bytes accessed | tf_op | source)
XLA Modules:
  0.0 893.8 jit_solution(8186871518844121848)
XLA Ops:
  34.1 11.7 %gather_fusion.2 = bf16[2048,768]{1,0:T(8,128)(2,1)} fusion(bf16[1025,768]{1,0:T(8,128)(2,1)} %concatenate.29, s32[2048]{0:T(1024)S(1)} %get-tuple-element.62), kind=kCustom, calls=%fused_computation.2 | custom fusion | bytes 6299648 | tf_op jit(solution)/shard_map/gather | solution.py:145
  54.9 10.7 %all-reduce.9 = (bf16[768]{0:T(1024)(128)(2,1)S(1)}, bf16[768]{0:T(1024)(128)(2,1)}) all-reduce(bf16[768]{0:T(1024)(128)(2,1)S(1)} %dynamic-update-slice, bf16[768]{0:T(1024)(128)(2,1)S(1)} %dynamic-update-slice.1), channel_id=1, replica_groups=mesh['expert'=8,'shard'=4] {'shard'}, use_global_device_ids=true, to_apply=%add.2 | all-reduce | flops 1536 | bytes 6144
  117.0 18.2 %all-gather.12.cloned.1.call-done = bf16[768,2048]{1,0:T(8,128)(2,1)} async-done(((bf16[768,512]{1,0:T(8,128)(2,1)}), bf16[768,2048]{1,0:T(8,128)(2,1)}) %all-gather.12.cloned.1.call-update) | async-done | bytes 3145744 | tf_op jit(solution)/shard_map/all_gather | solution.py:76
  141.1 39.6 %all-gather.14.cloned.1.call-done = bf16[768,2048]{1,0:T(8,128)(2,1)} async-done(((bf16[768,512]{1,0:T(8,128)(2,1)}), bf16[768,2048]{1,0:T(8,128)(2,1)}) %all-gather.14.cloned.1.call-update) | async-done | bytes 3145744 | tf_op jit(solution)/shard_map/all_gather | solution.py:77
  186.7 39.8 %all-gather.16.cloned.1.call-done = bf16[2048,768]{1,0:T(8,128)(2,1)} async-done(((bf16[512,768]{1,0:T(8,128)(2,1)}), bf16[2048,768]{1,0:T(8,128)(2,1)}) %all-gather.16.cloned.1.call-update) | async-done | bytes 3145744 | tf_op jit(solution)/shard_map/all_gather | solution.py:78
  226.4 10.0 %multiply_convert_fusion.4 = (bf16[512,2048]{1,0:T(8,128)(2,1)}, bf16[512,2048]{1,0:T(8,128)(2,1)S(1)}, bf16[512,2048]{1,0:T(8,128)(2,1)}) fusion(f32[512,2048]{1,0:T(8,128)} %fusion.62, f32[512,2048]{1,0:T(8,128)} %fusion.63, bf16[2048,768]{1,0:T(8,128)(2,1)} %all-gather.16.cloned.1.call-done, f32[512,768]{1,0:T(8,128)} %param.16), kind=kOutput, calls=%fused_computation.24 | convolution fusion | flops 1626734592 | bytes 19398656 | tf_op jit(solution)/shard_map/dot_general | solution.py:49
  243.3 11.3 %gather_fusion = bf16[2048,768]{1,0:T(8,128)(2,1)} fusion(bf16[513,768]{1,0:T(8,128)(2,1)} %concatenate.28, s32[2048]{0:T(1024)S(1)} %get-tuple-element.63), kind=kCustom, calls=%fused_computation | custom fusion | bytes 6299648 | tf_op jit(solution)/shard_map/gather | solution.py:145
  264.8 12.9 %fusion.9 = f32[2048,2048]{1,0:T(8,128)} fusion(bf16[2048,768]{1,0:T(8,128)(2,1)} %bitcast.18, bf16[1,2048,768]{2,1,0:T(8,128)(2,1)} %param.26), kind=kOutput, calls=%fused_computation.36 | convolution fusion | flops 6442450944 | bytes 23068672 | tf_op jit(solution)/shard_map/dot_general | solution.py:49
  277.8 53.1 %all-to-all-done = bf16[8,256,768]{2,1,0:T(8,128)(2,1)} async-done(((bf16[8,256,768]{2,1,0:T(8,128)(2,1)}), bf16[8,256,768]{2,1,0:T(8,128)(2,1)}, u32[]{:S(2)}, u32[]{:S(2)}) %all-to-all-start) | async-done | bytes 3145760 | tf_op jit(solution)/shard_map/all_to_all | solution.py:151
  330.9 12.7 %fusion.14 = f32[2048,2048]{1,0:T(8,128)} fusion(bf16[2048,768]{1,0:T(8,128)(2,1)} %bitcast.11, bf16[1,768,2048]{2,1,0:T(8,128)(2,1)} %param.25), kind=kOutput, calls=%fused_computation.41 | convolution fusion | flops 6442450944 | bytes 23068672 | tf_op jit(solution)/shard_map/dot_general | solution.py:49
  343.6 26.2 %multiply_convert_fusion.1 = (bf16[2048,2048]{1,0:T(8,128)(2,1)}, bf16[2048,2048]{1,0:T(8,128)(2,1)}, bf16[2048,2048]{1,0:T(8,128)(2,1)}) fusion(f32[2048,2048]{1,0:T(8,128)} %fusion.9, f32[2048,2048]{1,0:T(8,128)} %fusion.14, bf16[2048,768]{1,0:T(8,128)(2,1)} %bitcast.11, bf16[1,768,2048]{2,1,0:T(8,128)(2,1)S(1)} %copy-done), kind=kOutput, calls=%fused_computation.6 | convolution fusion | flops 6505365504 | bytes 65011712 | tf_op jit(solution)/shard_map/dot_general | solution.py:49
  369.8 10.4 %fusion.12 = f32[2048,768]{1,0:T(8,128)S(1)} fusion(bf16[2048,2048]{1,0:T(8,128)(2,1)} %get-tuple-element.43, bf16[1,768,2048]{2,1,0:T(8,128)(2,1)} %param.25), kind=kOutput, calls=%fused_computation.39 | convolution fusion | flops 6442450944 | bytes 17825792 | tf_op jit(solution)/shard_map/dot_general | solution.py:49
  404.0 59.5 %all-to-all-done.3 = bf16[8,256,768]{2,1,0:T(8,128)(2,1)S(1)} async-done(((bf16[8,256,768]{2,1,0:T(8,128)(2,1)}), bf16[8,256,768]{2,1,0:T(8,128)(2,1)S(1)}, u32[]{:S(2)}, u32[]{:S(2)}) %all-to-all-start.3) | async-done | bytes 3145760 | tf_op jit(solution)/shard_map/all_to_all | solution.py:192
  493.3 11.4 %multiply_reduce_fusion = (f32[12,512]{1,0:T(8,128)S(1)}, f32[12,512,512]{1,2,0:T(8,128)}) fusion(f32[12,512]{1,0:T(8,128)S(1)} %log_add_fusion, f32[12,512,512]{1,2,0:T(8,128)} %get-tuple-element.74, pred[512,512]{0,1:T(8,128)(4,1)S(1)} %copy-done.13, bf16[512,12,64]{0,2,1:T(8,128)(2,1)} %bitcast.128, bf16[512,12,64]{0,2,1:T(8,128)(2,1)S(1)} %bitcast.127), kind=kOutput, calls=%fused_computation.11 | convolution fusion | flops 418375680 | bytes 27049984 | tf_op jit(solution)/shard_map/qhd,khd->hqk/dot_general | solution.py:252
  506.1 10.1 %multiply_convert_fusion.3 = bf16[12,512,512]{1,2,0:T(8,128)(2,1)} fusion(f32[12,512,512]{1,2,0:T(8,128)} %get-tuple-element.79, f32[12,512]{1,0:T(8,128)S(1)} %get-tuple-element.78, f32[12,512]{1,0:T(8,128)S(1)} %log_add_fusion, f32[12,512,512]{1,2,0:T(8,128)S(1)} %bitcast.116, pred[512,512]{0,1:T(8,128)(4,1)S(1)} %copy-done.13), kind=kLoop, calls=%fused_computation.10 | loop fusion | flops 18874368 | bytes 31768576 | tf_op jit(solution)/shard_map/convert_element_type | solution.py:257
  533.2 12.2 %fusion.21 = bf16[1,768,2048]{2,1,0:T(8,128)(2,1)} fusion(bf16[2048,768]{1,0:T(8,128)(2,1)} %bitcast.11, bf16[2048,2048]{1,0:T(8,128)(2,1)} %get-tuple-element.42), kind=kOutput, calls=%fused_computation.51 | convolution fusion | flops 6444023808 | bytes 14680064 | tf_op jit(solution)/shard_map/dot_general | solution.py:49
  545.5 12.2 %fusion.22 = bf16[1,768,2048]{2,1,0:T(8,128)(2,1)} fusion(bf16[2048,768]{1,0:T(8,128)(2,1)} %bitcast.11, bf16[2048,2048]{1,0:T(8,128)(2,1)} %get-tuple-element.43), kind=kOutput, calls=%fused_computation.52 | convolution fusion | flops 6444023808 | bytes 14680064 | tf_op jit(solution)/shard_map/dot_general | solution.py:49
  557.7 11.6 %fusion.20 = bf16[1,2048,768]{2,1,0:T(8,128)(2,1)} fusion(bf16[2048,2048]{1,0:T(8,128)(2,1)} %get-tuple-element.44, bf16[2048,768]{1,0:T(8,128)(2,1)} %bitcast.18), kind=kOutput, calls=%fused_computation.50 | convolution fusion | flops 6444023808 | bytes 14680064 | tf_op jit(solution)/shard_map/dot_general | solution.py:49
  570.0 23.1 %reduce-scatter.9.cloned.1.call-done = bf16[192,2304]{1,0:T(8,128)(2,1)} async-done(((bf16[768,2304]{1,0:T(8,128)(2,1)}), bf16[192,2304]{1,0:T(8,128)(2,1)}) %reduce-scatter.9.cloned.1.call-update) | async-done | bytes 884752 | tf_op jit(solution)/shard_map/reduce_scatter | solution.py:279
  593.1 10.2 %convolution_convert_fusion.3 = bf16[2048,768]{1,0:T(8,128)(2,1)} fusion(bf16[2048,2048]{1,0:T(8,128)(2,1)} %get-tuple-element.44, bf16[1,2048,768]{2,1,0:T(8,128)(2,1)S(1)} %copy-done.57), kind=kOutput, calls=%fused_computation.31 | convolution fusion | flops 6444023808 | bytes 14680064 | tf_op jit(solution)/shard_map/dot_general | solution.py:49
  608.8 70.8 %all-to-all-done.1 = bf16[8,256,768]{2,1,0:T(8,128)(2,1)S(1)} async-done(((bf16[8,256,768]{2,1,0:T(8,128)(2,1)}), bf16[8,256,768]{2,1,0:T(8,128)(2,1)S(1)}, u32[]{:S(2)}, u32[]{:S(2)}) %all-to-all-start.1) | async-done | bytes 3145760 | tf_op jit(solution)/shard_map/all_to_all | solution.py:159
  704.8 13.6 %all-reduce.6 = (bf16[192]{0:T(256)(128)(2,1)S(1)}, bf16[192]{0:T(256)(128)(2,1)S(1)}) all-reduce(bf16[192]{0:T(256)(128)(2,1)S(1)} %dynamic-slice.3, bf16[192]{0:T(256)(128)(2,1)S(1)} %dynamic-slice.5), channel_id=1, replica_groups=mesh['expert'=8,'shard'=4] {'expert'}, use_global_device_ids=true, to_apply=%region_15.16 | all-reduce | flops 384 | bytes 1536 | tf_op jit(solution)/shard_map/psum | solution.py:294
  746.9 59.7 %all-reduce.12.cloned.1.call-done = (bf16[192,768]{1,0:T(8,128)(2,1)}, bf16[768,512]{1,0:T(8,128)(2,1)}, bf16[768,512]{1,0:T(8,128)(2,1)}, bf16[512,768]{1,0:T(8,128)(2,1)}) async-done(((bf16[192,768]{1,0:T(8,128)(2,1)}, bf16[768,512]{1,0:T(8,128)(2,1)}, bf16[768,512]{1,0:T(8,128)(2,1)}, bf16[512,768]{1,0:T(8,128)(2,1)}), (bf16[192,768]{1,0:T(8,128)(2,1)}, bf16[768,512]{1,0:T(8,128)(2,1)}, ...) | async-done | bytes 2654224 | tf_op jit(solution)/shard_map/psum | solution.py:293
  813.7 65.3 %all-gather.18.cloned.1.call-done = bf16[1536,2304]{1,0:T(8,128)(2,1)} async-done(((bf16[192,2304]{1,0:T(8,128)(2,1)}), bf16[1536,2304]{1,0:T(8,128)(2,1)}) %all-gather.18.cloned.1.call-update) | async-done | bytes 7077904 | tf_op jit(solution)/shard_map/all_gather | solution.py:290
  (281 shorter events, 260.3 us)
Async XLA Ops:
  7.2 336.4 %copy-start = (bf16[1,768,2048]{2,1,0:T(8,128)(2,1)S(1)}, bf16[1,768,2048]{2,1,0:T(8,128)(2,1)}, u32[]{:S(2)}) copy-start(bf16[1,768,2048]{2,1,0:T(8,128)(2,1)} %param.24) | copy-start | bytes 9437188
  7.2 63.1 %all-gather.8.cloned.1.call-start = ((), (), s32[]{:S(2)}) async-start(), calls=%async_computation.12 | async-start | bytes 4423680 | tf_op jit(solution)/shard_map/all_gather | solution.py:71
  7.9 103.8 %all-gather.10.cloned.1.call-start = ((), (), s32[]{:S(2)}) async-start(), calls=%async_computation.13 | async-start | bytes 1474560 | tf_op jit(solution)/shard_map/all_gather | solution.py:72
  8.7 126.5 %all-gather.12.cloned.1.call-start = ((), (), s32[]{:S(2)}) async-start(), calls=%async_computation.14 | async-start | bytes 3932160 | tf_op jit(solution)/shard_map/all_gather | solution.py:76
  9.4 171.3 %all-gather.14.cloned.1.call-start = ((), (), s32[]{:S(2)}) async-start(), calls=%async_computation.15 | async-start | bytes 3932160 | tf_op jit(solution)/shard_map/all_gather | solution.py:77
  45.9 208.8 %all-to-all-start.2 = ((bf16[8,256,768]{2,1,0:T(8,128)(2,1)}), bf16[8,256,768]{2,1,0:T(8,128)(2,1)}, u32[]{:S(2)}, u32[]{:S(2)}) async-start(bf16[8,256,768]{2,1,0:T(8,128)(2,1)} %bitcast.121), calls=%async_computation.2 | async-start | bytes 6291456 | tf_op jit(solution)/shard_map/all_to_all | solution.py:177
  52.5 173.9 %all-gather.16.cloned.1.call-start = ((), (), s32[]{:S(2)}) async-start(), calls=%async_computation.16 | async-start | bytes 3932160 | tf_op jit(solution)/shard_map/all_gather | solution.py:78
  53.1 516.3 %reduce-scatter.13.cloned.1.call-start = ((), (), s32[]{:S(2)}) async-start(), calls=%async_computation.19 | async-start | bytes 3932160 | tf_op jit(solution)/shard_map/reduce_scatter | solution.py:228
  68.6 36.3 %copy-start.12 = (pred[512,512]{0,1:T(8,128)(4,1)}, pred[512,512]{0,1:T(8,128)(4,1)S(1)}, u32[]{:S(2)}) copy-start(pred[512,512]{0,1:T(8,128)(4,1)S(1)} %fusion.29) | copy-start | bytes 786436
  70.2 45.1 %copy-start.43 = (f32[768]{0:T(1024)}, f32[768]{0:T(1024)S(1)}, u32[]{:S(2)}) copy-start(f32[768]{0:T(1024)S(1)} %convert_element_type.192) | copy-start | bytes 9220
  254.6 76.2 %all-to-all-start = ((bf16[8,256,768]{2,1,0:T(8,128)(2,1)}), bf16[8,256,768]{2,1,0:T(8,128)(2,1)}, u32[]{:S(2)}, u32[]{:S(2)}) async-start(bf16[8,256,768]{2,1,0:T(8,128)(2,1)} %bitcast.122), calls=%async_computation | async-start | bytes 6291456 | tf_op jit(solution)/shard_map/all_to_all | solution.py:151
  259.2 310.2 %reduce-scatter.15.cloned.1.call-start = ((), (), s32[]{:S(2)}) async-start(), calls=%async_computation.20 | async-start | bytes 3932160 | tf_op jit(solution)/shard_map/reduce_scatter | solution.py:231
  388.4 75.1 %all-to-all-start.3 = ((bf16[8,256,768]{2,1,0:T(8,128)(2,1)}), bf16[8,256,768]{2,1,0:T(8,128)(2,1)S(1)}, u32[]{:S(2)}, u32[]{:S(2)}) async-start(bf16[8,256,768]{2,1,0:T(8,128)(2,1)} %bitcast.132), calls=%async_computation.3 | async-start | bytes 6291456 | tf_op jit(solution)/shard_map/all_to_all | solution.py:192
  392.0 177.4 %reduce-scatter.17.cloned.1.call-start = ((), (), s32[]{:S(2)}) async-start(), calls=%async_computation.21 | async-start | bytes 3932160 | tf_op jit(solution)/shard_map/reduce_scatter | solution.py:234
  397.7 171.8 %reduce-scatter.11.cloned.1.call-start = ((), (), s32[]{:S(2)}) async-start(), calls=%async_computation.18 | async-start | bytes 1474560 | tf_op jit(solution)/shard_map/reduce_scatter | solution.py:282
  516.2 76.8 %reduce-scatter.9.cloned.1.call-start = ((), (), s32[]{:S(2)}) async-start(), calls=%async_computation.17 | async-start | bytes 4423680 | tf_op jit(solution)/shard_map/reduce_scatter | solution.py:279
  533.1 206.4 %reduce-scatter.19.cloned.1.call-start = ((), (), s32[]{:S(2)}) async-start(), calls=%async_computation.22 | async-start | bytes 3932160 | tf_op jit(solution)/shard_map/reduce_scatter | solution.py:198
  545.4 196.6 %reduce-scatter.21.cloned.1.call-start = ((), (), s32[]{:S(2)}) async-start(), calls=%async_computation.23 | async-start | bytes 3932160 | tf_op jit(solution)/shard_map/reduce_scatter | solution.py:201
  557.7 186.8 %reduce-scatter.23.cloned.1.call-start = ((), (), s32[]{:S(2)}) async-start(), calls=%async_computation.24 | async-start | bytes 3932160 | tf_op jit(solution)/shard_map/reduce_scatter | solution.py:204
  569.3 23.7 %copy-start.57 = (bf16[1,2048,768]{2,1,0:T(8,128)(2,1)S(1)}, bf16[1,2048,768]{2,1,0:T(8,128)(2,1)}, u32[]{:S(2)}) copy-start(bf16[1,2048,768]{2,1,0:T(8,128)(2,1)} %param.26) | copy-start | bytes 9437188
  569.3 237.3 %all-reduce.12.cloned.1.call-start = ((), (), s32[]{:S(2)}) async-start(), calls=%async_computation.26 | async-start | bytes 5308416 | tf_op jit(solution)/shard_map/psum | solution.py:293
  569.9 309.0 %all-gather.18.cloned.1.call-start = ((), (), s32[]{:S(2)}) async-start(), calls=%async_computation.25 | async-start | bytes 7962624 | tf_op jit(solution)/shard_map/all_gather | solution.py:290
  603.2 76.4 %all-to-all-start.1 = ((bf16[8,256,768]{2,1,0:T(8,128)(2,1)}), bf16[8,256,768]{2,1,0:T(8,128)(2,1)S(1)}, u32[]{:S(2)}, u32[]{:S(2)}) async-start(bf16[8,256,768]{2,1,0:T(8,128)(2,1)} %bitcast.133), calls=%async_computation.1 | async-start | bytes 6291456 | tf_op jit(solution)/shard_map/all_to_all | solution.py:159
  689.9 29.6 %copy-start.19 = (f32[512,2]{1,0:T(8,128)S(1)}, f32[512,2]{1,0:T(8,128)}, u32[]{:S(2)}) copy-start(f32[512,2]{1,0:T(8,128)} %copy-done.18) | copy-start | bytes 12292
  (65 other events, 370.0 us)
Sparse Core Ops, SparseCore 0:
  9.9 49.9 all-gather.7
  61.7 27.7 all-gather.9
  91.3 43.8 all-gather.11
  136.8 43.8 all-gather.13
  182.4 43.9 all-gather.15
  241.4 43.9 reduce-scatter.12
  288.3 43.9 reduce-scatter.14
  397.8 44.3 reduce-scatter.16
  516.3 26.4 reduce-scatter.10
  545.8 47.2 reduce-scatter.8
  596.0 43.9 reduce-scatter.18
  642.8 43.9 reduce-scatter.20
  689.8 44.0 reduce-scatter.22
  736.4 70.2 all-reduce.11
  808.1 70.7 all-gather.17
